TPU v7x, 32 devices: a whole 2x2x4 slice. The times are simulated.
32 devices in a mesh: prow: 4 (over y, core), pcol: 8 (over z, x).
Axes of the slice: x: 2, y: 2, z: 4, core: 2. Of those that a mesh axis runs over, the one named last changes fastest.
Arguments:
- ainv: bfloat16 [8192, 8192], P('prow', 'pcol'), may hold values from -6 to 6
- panels: bfloat16 [3, 8192, 128], P(None, ('prow', 'pcol')), may hold values from -0.0625 to 0.0625
- structure: int32 [3, 64], replicated, may hold values from 0 to 1, as said below
- dinv: float32 [3, 128, 128], replicated, may hold values from -6 to 6
- couple: bfloat16 [2, 128, 128], replicated, may hold values from -0.5 to 0.5
Outputs:
- inv_panels: float32 [3, 8192, 128], P(None, ('prow', 'pcol'))
- inv_parent: float32 [2, 128, 128], replicated
- inv_diag: float32 [3, 128, 128], replicated
Inputs may be any that keep to these rules, and one draw needn't show every extreme that they name: Entries are 0 or 1; a block in the structure of step k+1 is also in that of step k.
All inputs are finite; a program needn't handle non-finite values.
Results may differ from a plain program's by a relative error of at most 0.0003.
Values may be sent and summed in bfloat16 or wider, within the bound.
No kernel may reach another device: no remote copies, remote signals or barrier semaphores. Data moves between devices by JAX's collectives and lax.ppermute only.
A program may use at most 64 MiB of HBM per device.

v0:
```python
import jax
import jax.numpy as jnp
from jax import lax
from jax.sharding import PartitionSpec as P


def broadcast(value, axis, source):
    kept = jnp.where(lax.axis_index(axis) == source, value, 0).astype(value.dtype)
    return lax.psum(kept, axis)


def shards(ainv, panels, structure, dinv, couple):
    high = lax.Precision.HIGHEST
    n_col = lax.axis_size("pcol")
    seg_rows = panels.shape[1]
    width_cols = panels.shape[2]
    sections = panels.shape[0]
    col_span = ainv.shape[1]
    height = ainv.shape[0]
    flat_index = lax.axis_index("prow") * n_col + lax.axis_index("pcol")
    row_ids = flat_index * seg_rows + jnp.arange(seg_rows, dtype=jnp.int32)
    block_ids = jnp.arange(structure.shape[1], dtype=jnp.int32)
    onehot = (row_ids[:, None] // width_cols == block_ids[None, :]).astype(jnp.float32)
    live_rows = jnp.einsum("rb,kb->kr", onehot, structure.astype(jnp.float32))
    factor = panels * live_rows[:, :, None].astype(jnp.bfloat16)
    column = lax.axis_index("pcol")
    offset = column * col_span % height
    owner = column * col_span // height
    products = []
    for section in range(sections):
        gathered = lax.all_gather(factor[section], "pcol", axis=0, tiled=True)
        wanted = lax.dynamic_slice_in_dim(gathered, offset, col_span, 0)
        received = broadcast(wanted, "prow", owner)

        def single_term(row_start, row_count, panel_cols=received):
            return jnp.dot(ainv, panel_cols, preferred_element_type=jnp.float32)

        products.append(
            lax.psum_scatter(
                single_term(jnp.int32(0), seg_rows * lax.axis_size("pcol")),
                "pcol",
                scatter_dimension=0,
                tiled=True,
            )
        )
    factor_wide = factor.astype(jnp.float32)
    couple_wide = couple.astype(jnp.float32)
    first_block = -products[0] * live_rows[0][:, None]
    first_local = jnp.dot(factor_wide[0].T, first_block, precision=high)
    diag_now = dinv[0] - lax.psum(first_local, ("prow", "pcol"))
    blocks_out = [first_block]
    diag_out = [diag_now]
    cross_out = []
    for section in range(1, sections):
        previous = blocks_out[-1]
        current = (
            -(products[section] + jnp.dot(previous, couple_wide[section - 1], precision=high))
            * live_rows[section][:, None]
        )
        own_term = jnp.dot(factor_wide[section].T, current, precision=high)
        cross_term = jnp.dot(previous.T, factor_wide[section], precision=high)
        own_sum, cross_sum = lax.psum((own_term, cross_term), ("prow", "pcol"))
        cross = -(cross_sum + jnp.dot(diag_now, couple_wide[section - 1], precision=high))
        diag_now = (
            dinv[section] - own_sum - jnp.dot(couple_wide[section - 1].T, cross, precision=high)
        )
        blocks_out.append(current)
        cross_out.append(cross)
        diag_out.append(diag_now)
    return (jnp.stack(blocks_out), jnp.stack(cross_out), jnp.stack(diag_out))


def solution(mesh):
    return jax.shard_map(
        shards,
        mesh=mesh,
        in_specs=(P("prow", "pcol"), P(None, ("prow", "pcol"), None), P(), P(), P()),
        out_specs=(P(None, ("prow", "pcol"), None), P(), P()),
        check_vma=False,
    )
```

profile of v0, /device:TPU:8, one launch (start us, length us, event | category | flops | bytes accessed | tf_op | source)
XLA Modules:
  0.0 495.4 jit_solution(17148334694424355662)
XLA Ops:
  7.2 0.0 all-reduce.7.cloned.1.call-start
  7.3 0.9 fusion.45
  8.2 1.1 broadcast_multiply_fusion
  9.3 28.8 %all-gather = bf16[1,2048,128]{2,1,0:T(8,128)(2,1)S(1)} all-gather(bf16[1,256,128]{2,1,0:T(8,128)(2,1)S(1)} %get-tuple-element.14), channel_id=2, replica_groups=mesh['prow'=4,'pcol'=8] {'pcol'}, dimensions={1}, use_global_device_ids=true | all-gather | bytes 589824 | tf_op jit(solution)/shard_map/all_gather | solution.py:31
  38.0 31.6 %all-gather.2 = bf16[1,2048,128]{2,1,0:T(8,128)(2,1)S(1)} all-gather(bf16[1,256,128]{2,1,0:T(8,128)(2,1)S(1)} %get-tuple-element.15), channel_id=4, replica_groups=mesh['prow'=4,'pcol'=8] {'pcol'}, dimensions={1}, use_global_device_ids=true | all-gather | bytes 589824 | tf_op jit(solution)/shard_map/all_gather | solution.py:31
  69.6 0.8 select_bitcast_fusion.2
  70.4 0.8 select_bitcast_fusion
  71.2 31.1 %all-gather.1 = bf16[1,2048,128]{2,1,0:T(8,128)(2,1)S(1)} all-gather(bf16[1,256,128]{2,1,0:T(8,128)(2,1)S(1)} %get-tuple-element.16), channel_id=3, replica_groups=mesh['prow'=4,'pcol'=8] {'pcol'}, dimensions={1}, use_global_device_ids=true | all-gather | bytes 589824 | tf_op jit(solution)/shard_map/all_gather | solution.py:31
  102.3 0.8 select_bitcast_fusion.1
  103.0 0.0 all-reduce.7.cloned.1.call-update
  103.1 0.0 reduce-scatter.6.cloned.1.call-start
  103.1 39.1 %all-reduce.7.cloned.1.call-done = (bf16[1024,128]{1,0:T(8,128)(2,1)}, bf16[1024,128]{1,0:T(8,128)(2,1)}, bf16[1024,128]{1,0:T(8,128)(2,1)}) async-done(((bf16[1024,128]{1,0:T(8,128)(2,1)}, bf16[1024,128]{1,0:T(8,128)(2,1)}, bf16[1024,128]{1,0:T(8,128)(2,1)}), (bf16[1024,128]{1,0:T(8,128)(2,1)}, bf16[1024,128]{1,0:T(8,128)(2,1)}, bf16[1024,128]{1,0:T(8,128)(2,1)})) %all-reduce.7.cloned.1.call-update) | async-done | bytes 786448 | tf_op jit(solution)/shard_map/psum | solution.py:9
  142.2 0.0 copy-start.3
  142.2 4.8 convolution_bitcast_fusion.1
  147.0 0.0 reduce-scatter.6.cloned.1.call-update
  147.0 0.0 reduce-scatter.4.cloned.1.call-start
  147.1 0.0 copy-done.3
  147.1 4.7 convolution_bitcast_fusion.2
  151.8 0.0 reduce-scatter.4.cloned.1.call-update
  151.8 0.0 reduce-scatter.8.cloned.1.call-start
  151.9 0.0 copy-done.2
  151.9 0.0 copy-start.1
  151.9 4.8 convolution_bitcast_fusion
  156.7 0.0 reduce-scatter.8.cloned.1.call-update
  156.7 0.0 all-reduce.5.cloned.1.call-start
  156.7 54.9 %reduce-scatter.6.cloned.1.call-done = f32[256,128]{0,1:T(8,128)} async-done(((f32[2048,128]{0,1:T(8,128)}), f32[256,128]{0,1:T(8,128)}) %reduce-scatter.6.cloned.1.call-update) | async-done | bytes 131088 | tf_op jit(solution)/shard_map/reduce_scatter | solution.py:39
  211.7 67.1 %reduce-scatter.4.cloned.1.call-done = f32[256,128]{0,1:T(8,128)} async-done(((f32[2048,128]{0,1:T(8,128)}), f32[256,128]{0,1:T(8,128)}) %reduce-scatter.4.cloned.1.call-update) | async-done | bytes 131088 | tf_op jit(solution)/shard_map/reduce_scatter | solution.py:39
  278.8 0.0 copy-done
  278.8 1.2 fusion.2
  280.0 0.9 fusion.18
  280.9 0.8 fusion.12
  281.7 64.0 %reduce-scatter.8.cloned.1.call-done = f32[256,128]{0,1:T(8,128)} async-done(((f32[2048,128]{0,1:T(8,128)}), f32[256,128]{0,1:T(8,128)}) %reduce-scatter.8.cloned.1.call-update) | async-done | bytes 131088 | tf_op jit(solution)/shard_map/reduce_scatter | solution.py:39
  345.7 1.2 fusion.3
  346.9 0.9 fusion.14
  347.8 1.7 fusion.10
  349.5 1.8 fusion.9
  351.3 0.0 all-reduce.5.cloned.1.call-update
  351.3 0.9 fusion.11
  352.3 0.9 copy.12
  353.2 129.2 %all-reduce.5.cloned.1.call-done = (f32[128,128]{1,0:T(8,128)}, f32[128,128]{1,0:T(8,128)}, f32[128,128]{1,0:T(8,128)}, f32[128,128]{1,0:T(8,128)}, f32[128,128]{1,0:T(8,128)}) async-done(((f32[128,128]{1,0:T(8,128)}, f32[128,128]{1,0:T(8,128)}, f32[128,128]{1,0:T(8,128)}, f32[128,128]{1,0:T(8,128)}, f32[128,128]{1,0:T(8,128)}), (f32[128,128]{1,0:T(8,128)}, f32[128,128]{1,0:T(8,128)}, f32[128,128]{1,0:T(8,128)}, ...) | async-done | bytes 327696 | tf_op jit(solution)/shard_map/psum | solution.py:62
  482.4 0.0 copy-done.1
  482.4 0.8 fusion.30
  483.2 1.0 fusion.8
  484.3 1.1 fusion.7
  485.4 1.0 fusion.6
  486.4 1.1 fusion.5
  487.5 0.7 pad_maximum_fusion.2
  488.2 0.7 pad_maximum_fusion.1
  (6 shorter events, 0.1 us)
Async XLA Ops:
  7.2 135.0 %all-reduce.7.cloned.1.call-start = ((), (), s32[]{:S(2)}) async-start(), calls=%async_computation.7 | async-start | bytes 1572864 | tf_op jit(solution)/shard_map/psum | solution.py:9
  103.1 108.6 %reduce-scatter.6.cloned.1.call-start = ((), (), s32[]{:S(2)}) async-start(), calls=%async_computation.4 | async-start | bytes 1179648 | tf_op jit(solution)/shard_map/reduce_scatter | solution.py:39
  142.2 4.9 copy-start.3
  147.0 4.9 copy-start.2
  147.0 131.7 %reduce-scatter.4.cloned.1.call-start = ((), (), s32[]{:S(2)}) async-start(), calls=%async_computation.3 | async-start | bytes 1179648 | tf_op jit(solution)/shard_map/reduce_scatter | solution.py:39
  151.8 127.0 %copy-start = (bf16[2,128,128]{2,1,0:T(8,128)(2,1)S(1)}, bf16[2,128,128]{2,1,0:T(8,128)(2,1)}, u32[]{:S(2)}) copy-start(bf16[2,128,128]{2,1,0:T(8,128)(2,1)} %param.9) | copy-start | bytes 196612
  151.8 193.9 %reduce-scatter.8.cloned.1.call-start = ((), (), s32[]{:S(2)}) async-start(), calls=%async_computation.5 | async-start | bytes 1179648 | tf_op jit(solution)/shard_map/reduce_scatter | solution.py:39
  151.9 330.5 %copy-start.1 = (f32[3,128,128]{2,1,0:T(8,128)S(1)}, f32[3,128,128]{2,1,0:T(8,128)}, u32[]{:S(2)}) copy-start(f32[3,128,128]{2,1,0:T(8,128)} %param.8) | copy-start | bytes 589828
  156.7 325.7 %all-reduce.5.cloned.1.call-start = ((), (), s32[]{:S(2)}) async-start(), calls=%async_computation.6 | async-start | bytes 655360 | tf_op jit(solution)/shard_map/psum | solution.py:62
Sparse Core Ops, SparseCore 0:
  103.2 38.9 all-reduce.6
  147.2 64.4 reduce-scatter.5
  215.1 63.6 reduce-scatter.3
  282.0 63.6 reduce-scatter.7
  352.4 129.9 all-reduce.4
where the time goes:
time: 496 us; the launch traced here: 495 us
  waiting for transfers between devices  354 us (71%)
  blocking collectives  91.5 us (18%)
  matrix products  27.9 us (6%)
  between operations  13.9 us (3%)
  other arithmetic  6.52 us (1%)
    reduce_scatter x3, waiting for transfers between devices, shards(): lax.psum_scatter(single_term(jnp.int32(0), seg_rows * lax.axis_size('pcol...  186 us
    psum x1, waiting for transfers between devices, shards(): own_sum, cross_sum = lax.psum((own_term, cross_term), ('prow', 'pcol'))  129 us
    all_gather x3, blocking collectives, shards(): gathered = lax.all_gather(factor[section], 'pcol', axis=0, tiled=True)  91.5 us
    psum x1, waiting for transfers between devices, broadcast(): return lax.psum(kept, axis)  39.1 us
    dot_general x3, matrix products, single_term(): return jnp.dot(ainv, panel_cols, preferred_element_type=jnp.float32)  14.3 us
  transfers between devices with their start and end apart: 5, of which 5 were waited for; matrix products, arithmetic and copies ran while one was open for 3% of the time, Pallas kernels for 0%

commit v1 on v0

--- a/solution.py
+++ b/solution.py
@@ -59,7 +59,7 @@
         )
         own_term = jnp.dot(factor_wide[section].T, current, precision=high)
         cross_term = jnp.dot(previous.T, factor_wide[section], precision=high)
-        own_sum, cross_sum = lax.psum((own_term, cross_term), ("prow", "pcol"))
+        own_sum, cross_sum = lax.psum(lax.psum((own_term, cross_term), "pcol"), "prow")
         cross = -(cross_sum + jnp.dot(diag_now, couple_wide[section - 1], precision=high))
         diag_now = (
             dinv[section] - own_sum - jnp.dot(couple_wide[section - 1].T, cross, precision=high)

time: 496 us -> 596 us (1.20)
  waiting for transfers between devices: 354 us -> 452 us
    psum x1 -> x3, waiting for transfers between devices: 129 us -> 227 us  [the longest x1 126 us: shards(): diag_now = dinv[0] - lax.psum(first_local, ('prow', 'pcol'))]
  transfers between devices with their start and end apart: 5 -> 7, of which waited for: 5 -> 7; matrix products, arithmetic and copies ran while one was open for 3% -> 3% of each run, Pallas kernels for 0% -> 0%
where the time goes in v1:
time: 596 us; the launch traced here: 594 us
  waiting for transfers between devices  452 us (76%)
  blocking collectives  91.5 us (15%)
  matrix products  27.8 us (5%)
  between operations  14.3 us (2%)
  other arithmetic  6.52 us (1%)
    reduce_scatter x3, waiting for transfers between devices, shards(): lax.psum_scatter(single_term(jnp.int32(0), seg_rows * lax.axis_size('pcol...  186 us
    psum x1, waiting for transfers between devices, shards(): diag_now = dinv[0] - lax.psum(first_local, ('prow', 'pcol'))  126 us
    all_gather x3, blocking collectives, shards(): gathered = lax.all_gather(factor[section], 'pcol', axis=0, tiled=True)  91.5 us
    psum x1, waiting for transfers between devices, shards(): lax.psum((own_term, cross_term), 'pcol')  66.9 us
    psum x1, waiting for transfers between devices, broadcast(): return lax.psum(kept, axis)  39.1 us
    psum x1, waiting for transfers between devices, shards(): lax.psum(lax.psum((own_term, cross_term), 'pcol'), 'prow')  34.1 us
    dot_general x3, matrix products, single_term(): return jnp.dot(ainv, panel_cols, preferred_element_type=jnp.float32)  14.2 us
  transfers between devices with their start and end apart: 7, of which 7 were waited for; matrix products, arithmetic and copies ran while one was open for 3% of the time, Pallas kernels for 0%

profile of v1, /device:TPU:8, one launch (start us, length us, event | category | flops | bytes accessed | tf_op | source)
XLA Modules:
  0.0 593.7 jit_solution(14082303739751786607)
XLA Ops:
  7.2 0.0 all-reduce.14.cloned.1.call-start
  7.3 0.9 fusion.45
  8.2 1.1 broadcast_multiply_fusion
  9.3 28.8 %all-gather = bf16[1,2048,128]{2,1,0:T(8,128)(2,1)S(1)} all-gather(bf16[1,256,128]{2,1,0:T(8,128)(2,1)S(1)} %get-tuple-element.17), channel_id=2, replica_groups=mesh['prow'=4,'pcol'=8] {'pcol'}, dimensions={1}, use_global_device_ids=true | all-gather | bytes 589824 | tf_op jit(solution)/shard_map/all_gather | solution.py:31
  38.0 31.6 %all-gather.2 = bf16[1,2048,128]{2,1,0:T(8,128)(2,1)S(1)} all-gather(bf16[1,256,128]{2,1,0:T(8,128)(2,1)S(1)} %get-tuple-element.18), channel_id=4, replica_groups=mesh['prow'=4,'pcol'=8] {'pcol'}, dimensions={1}, use_global_device_ids=true | all-gather | bytes 589824 | tf_op jit(solution)/shard_map/all_gather | solution.py:31
  69.6 0.8 select_bitcast_fusion.2
  70.4 0.8 select_bitcast_fusion
  71.2 31.1 %all-gather.1 = bf16[1,2048,128]{2,1,0:T(8,128)(2,1)S(1)} all-gather(bf16[1,256,128]{2,1,0:T(8,128)(2,1)S(1)} %get-tuple-element.19), channel_id=3, replica_groups=mesh['prow'=4,'pcol'=8] {'pcol'}, dimensions={1}, use_global_device_ids=true | all-gather | bytes 589824 | tf_op jit(solution)/shard_map/all_gather | solution.py:31
  102.3 0.8 select_bitcast_fusion.1
  103.0 0.0 all-reduce.14.cloned.1.call-update
  103.0 0.0 reduce-scatter.6.cloned.1.call-start
  103.1 39.1 %all-reduce.14.cloned.1.call-done = (bf16[1024,128]{1,0:T(8,128)(2,1)}, bf16[1024,128]{1,0:T(8,128)(2,1)}, bf16[1024,128]{1,0:T(8,128)(2,1)}) async-done(((bf16[1024,128]{1,0:T(8,128)(2,1)}, bf16[1024,128]{1,0:T(8,128)(2,1)}, bf16[1024,128]{1,0:T(8,128)(2,1)}), (bf16[1024,128]{1,0:T(8,128)(2,1)}, bf16[1024,128]{1,0:T(8,128)(2,1)}, bf16[1024,128]{1,0:T(8,128)(2,1)})) %all-reduce.14.cloned.1.call-update) | async-done | bytes 786448 | tf_op jit(solution)/shard_map/psum | solution.py:9
  142.2 4.8 convolution_bitcast_fusion.1
  147.0 0.0 reduce-scatter.6.cloned.1.call-update
  147.0 0.0 reduce-scatter.4.cloned.1.call-start
  147.1 4.7 convolution_bitcast_fusion.2
  151.8 0.0 reduce-scatter.4.cloned.1.call-update
  151.8 0.0 reduce-scatter.8.cloned.1.call-start
  151.9 4.7 convolution_bitcast_fusion
  156.6 0.0 reduce-scatter.8.cloned.1.call-update
  156.6 0.0 all-reduce.10.cloned.1.call-start
  156.7 54.8 %reduce-scatter.6.cloned.1.call-done = f32[256,128]{0,1:T(8,128)} async-done(((f32[2048,128]{0,1:T(8,128)}), f32[256,128]{0,1:T(8,128)}) %reduce-scatter.6.cloned.1.call-update) | async-done | bytes 131088 | tf_op jit(solution)/shard_map/reduce_scatter | solution.py:39
  211.5 67.1 %reduce-scatter.4.cloned.1.call-done = f32[256,128]{0,1:T(8,128)} async-done(((f32[2048,128]{0,1:T(8,128)}), f32[256,128]{0,1:T(8,128)}) %reduce-scatter.4.cloned.1.call-update) | async-done | bytes 131088 | tf_op jit(solution)/shard_map/reduce_scatter | solution.py:39
  278.6 1.2 fusion.2
  279.8 0.9 fusion.18
  280.7 0.8 fusion.12
  281.5 64.1 %reduce-scatter.8.cloned.1.call-done = f32[256,128]{0,1:T(8,128)} async-done(((f32[2048,128]{0,1:T(8,128)}), f32[256,128]{0,1:T(8,128)}) %reduce-scatter.8.cloned.1.call-update) | async-done | bytes 131088 | tf_op jit(solution)/shard_map/reduce_scatter | solution.py:39
  345.6 1.2 fusion.3
  346.8 0.9 fusion.14
  347.7 1.7 fusion.10
  349.4 0.0 all-reduce.10.cloned.1.call-update
  349.4 0.0 all-reduce.8.cloned.1.call-start
  349.5 1.8 fusion.9
  351.2 0.0 all-reduce.8.cloned.1.call-update
  351.3 0.0 all-reduce.12.cloned.1.call-start
  351.3 0.9 fusion.11
  352.3 0.9 copy.12
  353.2 66.9 %all-reduce.10.cloned.1.call-done = (f32[128,128]{1,0:T(8,128)}, f32[128,128]{1,0:T(8,128)}, f32[128,128]{1,0:T(8,128)}, f32[128,128]{1,0:T(8,128)}) async-done(((f32[128,128]{1,0:T(8,128)}, f32[128,128]{1,0:T(8,128)}, f32[128,128]{1,0:T(8,128)}, f32[128,128]{1,0:T(8,128)}), (f32[128,128]{1,0:T(8,128)}, f32[128,128]{1,0:T(8,128)}, f32[128,128]{1,0:T(8,128)}, ...) | async-done | bytes 262160 | tf_op jit(solution)/shard_map/psum | solution.py:62
  420.1 0.0 all-reduce.12.cloned.1.call-update
  420.1 126.2 %all-reduce.8.cloned.1.call-done = f32[128,128]{1,0:T(8,128)} async-done(((f32[128,128]{1,0:T(8,128)}), f32[128,128]{1,0:T(8,128)}) %all-reduce.8.cloned.1.call-update) | async-done | bytes 65552 | tf_op jit(solution)/shard_map/psum | solution.py:50
  546.3 0.8 fusion.30
  547.2 34.1 %all-reduce.12.cloned.1.call-done = (f32[128,128]{1,0:T(8,128)}, f32[128,128]{1,0:T(8,128)}, f32[128,128]{1,0:T(8,128)}, f32[128,128]{1,0:T(8,128)}) async-done(((f32[128,128]{1,0:T(8,128)}, f32[128,128]{1,0:T(8,128)}, f32[128,128]{1,0:T(8,128)}, f32[128,128]{1,0:T(8,128)}), (f32[128,128]{1,0:T(8,128)}, f32[128,128]{1,0:T(8,128)}, f32[128,128]{1,0:T(8,128)}, ...) | async-done | bytes 262160 | tf_op jit(solution)/shard_map/psum | solution.py:62
  581.3 1.0 fusion.8
  582.3 1.1 fusion.7
  583.4 1.0 fusion.6
  584.4 1.1 fusion.5
  585.5 0.7 pad_maximum_fusion.2
  586.2 0.7 pad_maximum_fusion.1
  (12 shorter events, 0.1 us)
Async XLA Ops:
  7.2 135.0 %all-reduce.14.cloned.1.call-start = ((), (), s32[]{:S(2)}) async-start(), calls=%async_computation.9 | async-start | bytes 1572864 | tf_op jit(solution)/shard_map/psum | solution.py:9
  103.0 108.5 %reduce-scatter.6.cloned.1.call-start = ((), (), s32[]{:S(2)}) async-start(), calls=%async_computation.4 | async-start | bytes 1179648 | tf_op jit(solution)/shard_map/reduce_scatter | solution.py:39
  142.2 4.9 copy-start.3
  147.0 4.9 copy-start.2
  147.0 131.6 %reduce-scatter.4.cloned.1.call-start = ((), (), s32[]{:S(2)}) async-start(), calls=%async_computation.3 | async-start | bytes 1179648 | tf_op jit(solution)/shard_map/reduce_scatter | solution.py:39
  151.8 126.8 %copy-start = (bf16[2,128,128]{2,1,0:T(8,128)(2,1)S(1)}, bf16[2,128,128]{2,1,0:T(8,128)(2,1)}, u32[]{:S(2)}) copy-start(bf16[2,128,128]{2,1,0:T(8,128)(2,1)} %param.9) | copy-start | bytes 196612
  151.8 193.8 %reduce-scatter.8.cloned.1.call-start = ((), (), s32[]{:S(2)}) async-start(), calls=%async_computation.5 | async-start | bytes 1179648 | tf_op jit(solution)/shard_map/reduce_scatter | solution.py:39
  156.6 389.8 %copy-start.1 = (f32[3,128,128]{2,1,0:T(8,128)S(1)}, f32[3,128,128]{2,1,0:T(8,128)}, u32[]{:S(2)}) copy-start(f32[3,128,128]{2,1,0:T(8,128)} %param.8) | copy-start | bytes 589828
  156.6 263.5 %all-reduce.10.cloned.1.call-start = ((), (), s32[]{:S(2)}) async-start(), calls=%async_computation.7 | async-start | bytes 524288 | tf_op jit(solution)/shard_map/psum | solution.py:62
  349.4 196.9 %all-reduce.8.cloned.1.call-start = ((), (), s32[]{:S(2)}) async-start(), calls=%async_computation.6 | async-start | bytes 131072 | tf_op jit(solution)/shard_map/psum | solution.py:50
  351.3 230.0 %all-reduce.12.cloned.1.call-start = ((), (), s32[]{:S(2)}) async-start(), calls=%async_computation.8 | async-start | bytes 524288 | tf_op jit(solution)/shard_map/psum | solution.py:62
Sparse Core Ops, SparseCore 0:
  103.2 38.9 all-reduce.13
  147.1 64.3 reduce-scatter.5
  214.9 63.6 reduce-scatter.3
  281.8 63.6 reduce-scatter.7
  349.7 70.3 all-reduce.9
  425.5 120.7 all-reduce.7
  548.9 32.3 all-reduce.11
